TPU v7x, 256 devices: a whole 4x4x8 slice. The times are simulated.
256 devices in a mesh: grp: 8 (over z), blk: 32 (over y, x, core).
Axes of the slice: x: 4, y: 4, z: 8, core: 2. Of those that a mesh axis runs over, the one named last changes fastest.
Arguments:
- embeddings: bfloat16 [8, 2048, 1024], P('grp', 'blk'), may hold values from -72 to 72
- cluster_ids: int32 [8, 2048], P('grp', 'blk'), may hold values from 0 to 63, never falling along the last dimension, each value on 1 to 128 neighbouring positions
- block_list: int32 [8, 256, 2], P('grp', 'blk'), may hold values from 0 to 31, as said below
- block_counts: int32 [8, 32], P('grp', 'blk'), may hold values from 1 to 8, as said below
- pair_targets: float32 [8, 256, 4096], P('grp', 'blk'), may hold values from -6 to 6
- w_left: bfloat16 [1024, 512], replicated, may hold values from -0.125 to 0.125
- w_right: bfloat16 [1024, 512], replicated, may hold values from -0.125 to 0.125
- hidden_bias: float32 [512], replicated, may hold values from -3 to 3
- w_middle: bfloat16 [512, 128], replicated, may hold values from -0.25 to 0.25
- w_final: float32 [128], replicated, may hold values from -0.5 to 0.5
Outputs:
- grad_embeddings: float32 [8, 2048, 1024], P('grp', 'blk')
- grad_left: float32 [1024, 512], replicated
- grad_right: float32 [1024, 512], replicated
- grad_bias: float32 [512], replicated
- grad_middle: float32 [512, 128], replicated
- grad_final: float32 [128], replicated
Inputs may be any that keep to these rules, and one draw needn't show every extreme that they name: `block_list`: entries are panels of the device's own group; the column panel lies within one of the row panel. `block_counts`: slots of a device at and beyond its count are unused; in every group one device has exactly 8.
All inputs are finite; a program needn't handle non-finite values.
Results may differ from a plain program's by a relative error of at most 0.012.
Values may be sent and summed in bfloat16 or wider, within the bound.
No kernel may reach another device: no remote copies, remote signals or barrier semaphores. Data moves between devices by JAX's collectives and lax.ppermute only.
A program may use at most 128 MiB of HBM per device.

v0:
```python
import math
import jax
import jax.numpy as jnp
from jax import lax
from jax.sharding import PartitionSpec as P

PANEL = 64
B_DEV = 8


def silu_slope(value):
    sigmoid_value = jax.nn.sigmoid(value)
    return sigmoid_value * (1.0 + value * (1.0 - sigmoid_value))


def pair_block(
    left_rows,
    right_rows,
    left_ids,
    right_ids,
    row_start,
    col_start,
    pair_target,
    hidden_bias,
    w_middle,
    w_final,
):
    panel_rows = left_rows.shape[0]
    hidden_width = left_rows.shape[1]
    pre_hidden = (
        left_rows.astype(jnp.float32)[:, None, :]
        + right_rows.astype(jnp.float32)[None, :, :]
        + hidden_bias
    )
    hidden = (
        jax.nn.silu(pre_hidden).astype(jnp.bfloat16).reshape(panel_rows * panel_rows, hidden_width)
    )
    pre_upper = jnp.dot(hidden, w_middle, preferred_element_type=jnp.float32)
    upper_act = jax.nn.silu(pre_upper)
    predicted = jnp.sum(upper_act * w_final, axis=1)
    left_pos = row_start + jnp.arange(panel_rows, dtype=jnp.int32)
    right_pos = col_start + jnp.arange(panel_rows, dtype=jnp.int32)
    same_cluster = (left_ids[:, None] == right_ids[None, :]) & (
        left_pos[:, None] != right_pos[None, :]
    )
    residual = jnp.where(same_cluster.reshape(-1), predicted - pair_target, 0.0)
    pair_slope = 16.0 * residual
    grad_final = jnp.sum(upper_act * pair_slope[:, None], axis=0)
    grad_second = (pair_slope[:, None] * w_final[None, :] * silu_slope(pre_upper)).astype(
        jnp.bfloat16
    )
    grad_middle = lax.dot_general(
        hidden, grad_second, (((0,), (0,)), ((), ())), preferred_element_type=jnp.float32
    )
    grad_hidden = lax.dot_general(
        grad_second, w_middle, (((1,), (1,)), ((), ())), preferred_element_type=jnp.float32
    )
    grad_first = grad_hidden.reshape(panel_rows, panel_rows, hidden_width) * silu_slope(pre_hidden)
    return (
        jnp.sum(grad_first, axis=1),
        jnp.sum(grad_first, axis=0),
        jnp.sum(grad_first, axis=(0, 1)),
        grad_middle,
        grad_final,
    )


def local(
    embeddings,
    cluster_ids,
    block_list,
    block_counts,
    pair_targets,
    w_left,
    w_right,
    hidden_bias,
    w_middle,
    w_final,
):
    local_emb = embeddings[0]
    whole_emb, group_ids = (
        lax.all_gather(embeddings, "blk", axis=1, tiled=True),
        lax.all_gather(cluster_ids, "blk", axis=1, tiled=True),
    )
    whole_emb = whole_emb[0]

    def fetch_panels(row_start, col_start):
        row_emb = lax.dynamic_slice_in_dim(whole_emb, row_start, PANEL, 0)
        col_emb = lax.dynamic_slice_in_dim(whole_emb, col_start, PANEL, 0)
        return (
            jnp.dot(row_emb, w_left, preferred_element_type=jnp.float32).astype(jnp.bfloat16),
            jnp.dot(col_emb, w_right, preferred_element_type=jnp.float32).astype(jnp.bfloat16),
        )

    group_ids = group_ids[0]
    local_blocks = block_list[0]
    local_targets = pair_targets[0]
    molecules = group_ids.shape[0]
    hidden_width = w_left.shape[1]

    def slot_step(slot, carry):
        part_left, part_right, sum_bias, sum_middle, sum_final = carry
        entry = lax.dynamic_index_in_dim(local_blocks, slot, 0, keepdims=False)
        row_start = entry[0] * PANEL
        col_start = entry[1] * PANEL
        pair_target = lax.dynamic_index_in_dim(local_targets, slot, 0, keepdims=False)
        left_rows, right_rows = fetch_panels(row_start, col_start)
        grad_rows, grad_cols, grad_bias, grad_middle, grad_final = pair_block(
            left_rows,
            right_rows,
            lax.dynamic_slice_in_dim(group_ids, row_start, PANEL, 0),
            lax.dynamic_slice_in_dim(group_ids, col_start, PANEL, 0),
            row_start,
            col_start,
            pair_target,
            hidden_bias,
            w_middle,
            w_final,
        )
        current = lax.dynamic_slice_in_dim(part_left, row_start, PANEL, 0)
        part_left = lax.dynamic_update_slice_in_dim(part_left, current + grad_rows, row_start, 0)
        current = lax.dynamic_slice_in_dim(part_right, col_start, PANEL, 0)
        part_right = lax.dynamic_update_slice_in_dim(part_right, current + grad_cols, col_start, 0)
        return (
            part_left,
            part_right,
            sum_bias + grad_bias,
            sum_middle + grad_middle,
            sum_final + grad_final,
        )

    empty = jnp.zeros((molecules, hidden_width), jnp.float32)
    start_state = (
        empty,
        empty,
        jnp.zeros((hidden_width,), jnp.float32),
        jnp.zeros(w_middle.shape, jnp.float32),
        jnp.zeros(w_final.shape, jnp.float32),
    )
    part_left, part_right, sum_bias, sum_middle, sum_final = lax.fori_loop(
        0, block_counts[0, 0], slot_step, start_state
    )
    rounded_left = part_left.astype(jnp.bfloat16)
    rounded_right = part_right.astype(jnp.bfloat16)
    own_left, own_right = (
        lax.psum_scatter(
            rounded_left.astype(jnp.float32).astype(jnp.bfloat16),
            "blk",
            scatter_dimension=0,
            tiled=True,
        ).astype(jnp.float32),
        lax.psum_scatter(
            rounded_right.astype(jnp.float32).astype(jnp.bfloat16),
            "blk",
            scatter_dimension=0,
            tiled=True,
        ).astype(jnp.float32),
    )
    left_grad = own_left.astype(jnp.bfloat16)
    right_grad = own_right.astype(jnp.bfloat16)
    grad_local = jnp.dot(left_grad, w_left.T, preferred_element_type=jnp.float32) + jnp.dot(
        right_grad, w_right.T, preferred_element_type=jnp.float32
    )
    weight_left = lax.dot_general(
        local_emb, left_grad, (((0,), (0,)), ((), ())), preferred_element_type=jnp.float32
    )
    weight_right = lax.dot_general(
        local_emb, right_grad, (((0,), (0,)), ((), ())), preferred_element_type=jnp.float32
    )
    summed = lax.psum((weight_left, weight_right, sum_bias, sum_middle, sum_final), ("grp", "blk"))
    devices = lax.axis_size("grp") * lax.axis_size("blk")
    scale = 1.0 / math.sqrt(devices * B_DEV * PANEL)
    return (
        grad_local[None],
        summed[0] * scale,
        summed[1] * scale,
        summed[2] * scale,
        summed[3] * scale,
        summed[4] * scale,
    )


def solution(mesh):
    return jax.shard_map(
        local,
        mesh=mesh,
        in_specs=(
            P("grp", "blk", None),
            P("grp", "blk"),
            P("grp", "blk", None),
            P("grp", "blk"),
            P("grp", "blk", None),
            P(),
            P(),
            P(),
            P(),
            P(),
        ),
        out_specs=(P("grp", "blk", None), P(), P(), P(), P(), P()),
        check_vma=False,
    )
```

profile of v0, /device:TPU:2, one launch (start us, length us, event | category | flops | bytes accessed | tf_op | source)
XLA Modules:
  0.0 784.3 jit_solution(16809696372307641489)
XLA Ops:
  7.2 0.7 all-gather.2.cloned.1.call-update
  7.9 1.3 dynamic-slice
  9.9 0.8 bitcast_dynamic-update-slice_fusion
  10.7 15.9 %all-reduce = s32[2048]{0:T(1024)S(1)} all-reduce(s32[2048]{0:T(1024)S(1)} %bitcast_dynamic-update-slice_fusion), channel_id=1, replica_groups=mesh['grp'=8,'blk'=32] {'blk'}, use_global_device_ids=true, to_apply=%add | all-reduce | flops 2048 | bytes 16384 | tf_op jit(solution)/shard_map/squeeze | solution.py:95
  26.5 37.7 %all-gather.2.cloned.1.call-done = bf16[1,2048,1024]{2,1,0:T(8,128)(2,1)} async-done(((bf16[1,64,1024]{2,1,0:T(8,128)(2,1)}), bf16[1,2048,1024]{2,1,0:T(8,128)(2,1)}) %all-gather.2.cloned.1.call-update) | async-done | bytes 4194320 | tf_op jit(solution)/shard_map/all_gather | solution.py:82
  64.3 2.5 broadcast_in_dim.14
  66.7 2.5 broadcast_in_dim.14.clone
  69.2 0.7 broadcast_in_dim.16
  70.0 60.5 %while.18 = (s32[]{:T(128)}, f32[2048,512]{1,0:T(8,128)}, f32[2048,512]{1,0:T(8,128)}, f32[512]{0:T(512)S(1)}, f32[512,128]{1,0:T(8,128)}, /*index=5*/f32[128]{0...) while((s32[]{:T(128)}, f32[2048,512]{1,0:T(8,128)}, ...), condition=%wide.region_6.7_spmd, body=%wide.region_0.6_spmd.sunk | while | flops 1822642304 | bytes 153014800 | solution.py:140
  71.9 1.2 fusion.50
  73.7 1.6 fusion.49
  75.3 1.1 broadcast_add_fusion.2
  76.5 3.4 multiply_convert_fusion.7
  79.9 1.3 multiply_reduce_fusion.6
  81.2 0.6 copy-done.2
  82.1 0.9 constant_dynamic-slice_fusion.5
  83.1 5.0 convolution_add_fusion.3
  88.1 5.3 multiply_reduce_fusion.7
  93.4 3.9 fusion.52
  97.3 1.7 add_dynamic-update-slice_fusion.3
  99.1 0.7 multiply_reduce_fusion.8
  100.5 0.5 fusion.48
  101.7 1.2 fusion.50
  103.6 1.6 fusion.49
  105.2 1.1 broadcast_add_fusion.2
  106.3 3.4 multiply_convert_fusion.7
  109.7 1.3 multiply_reduce_fusion.6
  111.1 0.6 copy-done.2
  112.0 0.9 constant_dynamic-slice_fusion.5
  112.9 5.0 convolution_add_fusion.3
  118.0 5.3 multiply_reduce_fusion.7
  123.2 3.9 fusion.52
  127.2 1.7 add_dynamic-update-slice_fusion.3
  128.9 0.7 multiply_reduce_fusion.8
  130.5 3.8 convert_element_type.34
  134.3 3.8 convert_element_type.33
  138.2 261.0 %reduce-scatter.5.cloned.1.call-done = bf16[64,512]{1,0:T(8,128)(2,1)} async-done(((bf16[2048,512]{1,0:T(8,128)(2,1)}), bf16[64,512]{1,0:T(8,128)(2,1)}) %reduce-scatter.5.cloned.1.call-update) | async-done | bytes 65552 | tf_op jit(solution)/shard_map/reduce_scatter | solution.py:152
  399.2 2.6 convolution_bitcast_fusion
  401.8 87.8 %reduce-scatter.3.cloned.1.call-done = bf16[64,512]{1,0:T(8,128)(2,1)} async-done(((bf16[2048,512]{1,0:T(8,128)(2,1)}), bf16[64,512]{1,0:T(8,128)(2,1)}) %reduce-scatter.3.cloned.1.call-update) | async-done | bytes 65552 | tf_op jit(solution)/shard_map/reduce_scatter | solution.py:146
  489.6 2.7 convolution_bitcast_fusion.1
  492.3 73.9 %all-reduce.1 = (f32[512]{0:T(512)S(1)}, f32[128]{0:T(128)S(1)}) all-reduce(f32[512]{0:T(512)S(1)} %get-tuple-element.95, f32[128]{0:T(128)S(1)} %get-tuple-element.97), channel_id=1, replica_groups=mesh['grp'=8,'blk'=32] {'grp','blk'}, use_global_device_ids=true, to_apply=%region_11.12 | all-reduce | flops 640 | bytes 5120 | tf_op jit(solution)/shard_map/psum | solution.py:170
  566.7 0.6 broadcast_multiply_fusion.3
  567.7 2.4 fusion.8
  570.1 198.0 %all-reduce.5.cloned.1.call-done = (f32[1024,512]{0,1:T(8,128)}, f32[1024,512]{0,1:T(8,128)}, f32[512,128]{1,0:T(8,128)}) async-done(((f32[1024,512]{0,1:T(8,128)}, f32[1024,512]{0,1:T(8,128)}, f32[512,128]{1,0:T(8,128)}), (f32[1024,512]{0,1:T(8,128)}, f32[1024,512]{0,1:T(8,128)}, f32[512,128]{1,0:T(8,128)})) %all-reduce.5.cloned.1.call-update) | async-done | bytes 4456464 | tf_op jit(solution)/shard_map/psum | solution.py:170
  768.1 4.2 broadcast_multiply_fusion
  772.3 2.9 copy.16
  775.2 1.8 copy.17
  777.0 0.7 broadcast_multiply_fusion.2
  (65 shorter events, 2.5 us)
Async XLA Ops:
  7.2 57.1 %all-gather.2.cloned.1.call-start = ((), (), s32[]{:S(2)}) async-start(), calls=%async_computation.2 | async-start | bytes 4325376 | tf_op jit(solution)/shard_map/all_gather | solution.py:82
  7.9 391.3 %reduce-scatter.5.cloned.1.call-start = ((), (), s32[]{:S(2)}) async-start(), calls=%async_computation.4 | async-start | bytes 2162688 | tf_op jit(solution)/shard_map/reduce_scatter | solution.py:152
  64.2 5.7 copy-start.3
  64.3 5.7 copy-start.8
  64.3 5.7 copy-start.9
  64.3 5.7 copy-start.12
  76.5 3.4 copy-start
  76.5 3.4 copy-start.10
  79.9 2.0 copy-start.2
  83.1 5.1 copy-start.1
  83.1 5.1 copy-start.11
  106.3 3.4 copy-start
  106.3 3.4 copy-start.10
  109.7 2.0 copy-start.2
  112.9 5.1 copy-start.1
  112.9 5.1 copy-start.11
  134.3 355.3 %reduce-scatter.3.cloned.1.call-start = ((), (), s32[]{:S(2)}) async-start(), calls=%async_computation.3 | async-start | bytes 2162688 | tf_op jit(solution)/shard_map/reduce_scatter | solution.py:146
  134.3 264.9 %copy-start.4 = (bf16[1,64,1024]{2,1,0:T(8,128)(2,1)S(1)}, bf16[1,64,1024]{2,1,0:T(8,128)(2,1)}, u32[]{:S(2)}) copy-start(bf16[1,64,1024]{2,1,0:T(8,128)(2,1)} %param.12) | copy-start | bytes 393220
  138.2 629.9 %all-reduce.5.cloned.1.call-start = ((), (), s32[]{:S(2)}) async-start(), calls=%async_computation.5 | async-start | bytes 8912896 | tf_op jit(solution)/shard_map/psum | solution.py:170
  401.8 165.9 %copy-start.5 = (bf16[64,512]{1,0:T(8,128)(2,1)S(1)}, bf16[64,512]{1,0:T(8,128)(2,1)}, u32[]{:S(2)}) copy-start(bf16[64,512]{1,0:T(8,128)(2,1)} %reduce-scatter.5.cloned.1.call-done) | copy-start | bytes 196612
  489.6 77.7 %copy-start.7 = (bf16[64,512]{1,0:T(8,128)(2,1)S(1)}, bf16[64,512]{1,0:T(8,128)(2,1)}, u32[]{:S(2)}) copy-start(bf16[64,512]{1,0:T(8,128)(2,1)} %reduce-scatter.3.cloned.1.call-done) | copy-start | bytes 196612
  772.3 4.7 copy-start.6
Sparse Core Ops, SparseCore 0:
  10.5 53.6 all-gather.1
  134.4 264.7 reduce-scatter.4
  403.6 85.9 reduce-scatter.2
  495.8 272.2 all-reduce.4
where the time goes:
time: 786 us; the launch traced here: 784 us
  waiting for transfers between devices  585 us (74%)
  blocking collectives  89.8 us (11%)
  matrix products  37 us (5%)
  other arithmetic  35.6 us (5%)
  local copies, waits for them, and re-layouts  17.1 us (2%)
  between operations  14.5 us (2%)
    reduce_scatter x1, waiting for transfers between devices, local(): lax.psum_scatter(rounded_right.astype(jnp.float32).astype(jnp.bfloat16),...  261 us
    psum x1, waiting for transfers between devices, local(): lax.psum((weight_left, weight_right, sum_bias, sum_middle, sum_final), ('...  198 us
    reduce_scatter x1, waiting for transfers between devices, local(): lax.psum_scatter(rounded_left.astype(jnp.float32).astype(jnp.bfloat16), '...  87.8 us
    psum x1, blocking collectives, local(): lax.psum((weight_left, weight_right, sum_bias, sum_middle, sum_final), ('...  73.9 us
    all_gather x1, waiting for transfers between devices, local(): lax.all_gather(embeddings, 'blk', axis=1, tiled=True)  37.7 us
    squeeze x1, blocking collectives, local(): group_ids = group_ids[0]  15.9 us
  transfers between devices with their start and end apart: 4, of which 4 were waited for; matrix products, arithmetic and copies ran while one was open for 2% of the time, Pallas kernels for 0%

commit v1 on v0

--- a/solution.py
+++ b/solution.py
@@ -167,7 +167,8 @@
     weight_right = lax.dot_general(
         local_emb, right_grad, (((0,), (0,)), ((), ())), preferred_element_type=jnp.float32
     )
-    summed = lax.psum((weight_left, weight_right, sum_bias, sum_middle, sum_final), ("grp", "blk"))
+    partial = lax.psum((weight_left, weight_right, sum_bias, sum_middle, sum_final), "blk")
+    summed = lax.psum(partial, "grp")
     devices = lax.axis_size("grp") * lax.axis_size("blk")
     scale = 1.0 / math.sqrt(devices * B_DEV * PANEL)
     return (

time: 786 us -> 751 us (0.955)
  waiting for transfers between devices: 585 us -> 544 us
    psum x1 -> x2, waiting for transfers between devices: 198 us -> 157 us  [the longest x1 123 us: local(): lax.psum((weight_left, weight_right, sum_bias, sum_middle, sum_final), 'b...]
    psum x1 -> x2, blocking collectives: 73.9 us -> 79.6 us  [the longest x1 61.8 us: local(): lax.psum((weight_left, weight_right, sum_bias, sum_middle, sum_final), 'b...]
  transfers between devices with their start and end apart: 4 -> 5, of which waited for: 4 -> 5; matrix products, arithmetic and copies ran while one was open for 2% -> 2% of each run, Pallas kernels for 0% -> 0%
where the time goes in v1:
time: 751 us; the launch traced here: 749 us
  waiting for transfers between devices  544 us (72%)
  blocking collectives  95.5 us (13%)
  matrix products  36.9 us (5%)
  other arithmetic  35.6 us (5%)
  local copies, waits for them, and re-layouts  17.1 us (2%)
  between operations  14.5 us (2%)
    reduce_scatter x1, waiting for transfers between devices, local(): lax.psum_scatter(rounded_right.astype(jnp.float32).astype(jnp.bfloat16),...  261 us
    psum x1, waiting for transfers between devices, local(): lax.psum((weight_left, weight_right, sum_bias, sum_middle, sum_final), 'b...  123 us
    reduce_scatter x1, waiting for transfers between devices, local(): lax.psum_scatter(rounded_left.astype(jnp.float32).astype(jnp.bfloat16), '...  87.8 us
    psum x1, blocking collectives, local(): lax.psum((weight_left, weight_right, sum_bias, sum_middle, sum_final), 'b...  61.8 us
    all_gather x1, waiting for transfers between devices, local(): lax.all_gather(embeddings, 'blk', axis=1, tiled=True)  37.7 us
    psum x1, waiting for transfers between devices, local(): summed = lax.psum(partial, 'grp')  33.4 us
    psum x1, blocking collectives, local(): summed = lax.psum(partial, 'grp')  17.9 us
    squeeze x1, blocking collectives, local(): group_ids = group_ids[0]  15.9 us
  transfers between devices with their start and end apart: 5, of which 5 were waited for; matrix products, arithmetic and copies ran while one was open for 2% of the time, Pallas kernels for 0%

profile of v1, /device:TPU:2, one launch (start us, length us, event | category | flops | bytes accessed | tf_op | source)
XLA Modules:
  0.0 748.6 jit_solution(13064960240380945875)
XLA Ops:
  7.2 0.7 all-gather.2.cloned.1.call-update
  7.9 1.3 dynamic-slice
  9.9 0.8 bitcast_dynamic-update-slice_fusion
  10.7 15.9 %all-reduce = s32[2048]{0:T(1024)S(1)} all-reduce(s32[2048]{0:T(1024)S(1)} %bitcast_dynamic-update-slice_fusion), channel_id=1, replica_groups=mesh['grp'=8,'blk'=32] {'blk'}, use_global_device_ids=true, to_apply=%add | all-reduce | flops 2048 | bytes 16384 | tf_op jit(solution)/shard_map/squeeze | solution.py:95
  26.5 37.7 %all-gather.2.cloned.1.call-done = bf16[1,2048,1024]{2,1,0:T(8,128)(2,1)} async-done(((bf16[1,64,1024]{2,1,0:T(8,128)(2,1)}), bf16[1,2048,1024]{2,1,0:T(8,128)(2,1)}) %all-gather.2.cloned.1.call-update) | async-done | bytes 4194320 | tf_op jit(solution)/shard_map/all_gather | solution.py:82
  64.3 2.5 broadcast_in_dim.14
  66.7 2.5 broadcast_in_dim.14.clone
  69.2 0.7 broadcast_in_dim.16
  70.0 60.5 %while.18 = (s32[]{:T(128)}, f32[2048,512]{1,0:T(8,128)}, f32[2048,512]{1,0:T(8,128)}, f32[512]{0:T(512)S(1)}, f32[512,128]{1,0:T(8,128)}, /*index=5*/f32[128]{0...) while((s32[]{:T(128)}, f32[2048,512]{1,0:T(8,128)}, ...), condition=%wide.region_6.7_spmd, body=%wide.region_0.6_spmd.sunk | while | flops 1822642304 | bytes 153014800 | solution.py:140
  71.9 1.2 fusion.50
  73.7 1.6 fusion.49
  75.3 1.1 broadcast_add_fusion.2
  76.5 3.4 multiply_convert_fusion.7
  79.9 1.3 multiply_reduce_fusion.6
  81.2 0.6 copy-done.2
  82.1 0.9 constant_dynamic-slice_fusion.5
  83.1 5.0 convolution_add_fusion.3
  88.1 5.3 multiply_reduce_fusion.7
  93.4 3.9 fusion.52
  97.3 1.7 add_dynamic-update-slice_fusion.3
  99.1 0.7 multiply_reduce_fusion.8
  101.7 1.2 fusion.50
  103.6 1.6 fusion.49
  105.2 1.1 broadcast_add_fusion.2
  106.3 3.4 multiply_convert_fusion.7
  109.7 1.3 multiply_reduce_fusion.6
  111.1 0.6 copy-done.2
  112.0 0.9 constant_dynamic-slice_fusion.5
  112.9 5.0 convolution_add_fusion.3
  118.0 5.3 multiply_reduce_fusion.7
  123.2 3.9 fusion.52
  127.2 1.7 add_dynamic-update-slice_fusion.3
  128.9 0.7 multiply_reduce_fusion.8
  130.5 3.8 convert_element_type.34
  134.3 3.8 convert_element_type.33
  138.2 261.0 %reduce-scatter.5.cloned.1.call-done = bf16[64,512]{1,0:T(8,128)(2,1)} async-done(((bf16[2048,512]{1,0:T(8,128)(2,1)}), bf16[64,512]{1,0:T(8,128)(2,1)}) %reduce-scatter.5.cloned.1.call-update) | async-done | bytes 65552 | tf_op jit(solution)/shard_map/reduce_scatter | solution.py:152
  399.2 2.6 convolution_bitcast_fusion
  401.8 87.8 %reduce-scatter.3.cloned.1.call-done = bf16[64,512]{1,0:T(8,128)(2,1)} async-done(((bf16[2048,512]{1,0:T(8,128)(2,1)}), bf16[64,512]{1,0:T(8,128)(2,1)}) %reduce-scatter.3.cloned.1.call-update) | async-done | bytes 65552 | tf_op jit(solution)/shard_map/reduce_scatter | solution.py:146
  489.6 2.6 convolution_bitcast_fusion.1
  492.3 123.1 %all-reduce.8.cloned.1.call-done = (f32[1024,512]{0,1:T(8,128)}, f32[1024,512]{0,1:T(8,128)}, f32[512,128]{1,0:T(8,128)}) async-done(((f32[1024,512]{0,1:T(8,128)}, f32[1024,512]{0,1:T(8,128)}, f32[512,128]{1,0:T(8,128)}), (f32[1024,512]{0,1:T(8,128)}, f32[1024,512]{0,1:T(8,128)}, f32[512,128]{1,0:T(8,128)})) %all-reduce.8.cloned.1.call-update) | async-done | bytes 4456464 | tf_op jit(solution)/shard_map/psum | solution.py:170
  615.4 61.8 %all-reduce.1 = (f32[512]{0:T(512)S(1)}, f32[128]{0:T(128)S(1)}) all-reduce(f32[512]{0:T(512)S(1)} %get-tuple-element.95, f32[128]{0:T(128)S(1)} %get-tuple-element.97), channel_id=1, replica_groups=mesh['grp'=8,'blk'=32] {'blk'}, use_global_device_ids=true, to_apply=%region_13.14 | all-reduce | flops 640 | bytes 5120 | tf_op jit(solution)/shard_map/psum | solution.py:170
  677.2 17.9 %all-reduce.3 = (f32[512]{0:T(512)S(1)}, f32[128]{0:T(128)S(1)}) all-reduce(f32[512]{0:T(512)S(1)} %get-tuple-element.138, f32[128]{0:T(128)S(1)} %get-tuple-element.139), channel_id=1, replica_groups=mesh['grp'=8,'blk'=32] {'grp'}, use_global_device_ids=true, to_apply=%region_14.15 | all-reduce | flops 640 | bytes 5120 | tf_op jit(solution)/shard_map/psum | solution.py:171
  696.6 2.4 fusion.8
  698.9 33.4 %all-reduce.10.cloned.1.call-done = (f32[1024,512]{0,1:T(8,128)}, f32[1024,512]{0,1:T(8,128)}, f32[512,128]{1,0:T(8,128)}) async-done(((f32[1024,512]{0,1:T(8,128)}, f32[1024,512]{0,1:T(8,128)}, f32[512,128]{1,0:T(8,128)}), (f32[1024,512]{0,1:T(8,128)}, f32[1024,512]{0,1:T(8,128)}, f32[512,128]{1,0:T(8,128)})) %all-reduce.10.cloned.1.call-update) | async-done | bytes 4456464 | tf_op jit(solution)/shard_map/psum | solution.py:171
  732.3 4.2 broadcast_multiply_fusion
  736.6 2.9 copy.16
  739.5 1.8 copy.17
  741.3 0.7 broadcast_multiply_fusion.2
  (69 shorter events, 3.6 us)
Async XLA Ops:
  7.2 57.1 %all-gather.2.cloned.1.call-start = ((), (), s32[]{:S(2)}) async-start(), calls=%async_computation.2 | async-start | bytes 4325376 | tf_op jit(solution)/shard_map/all_gather | solution.py:82
  7.9 391.3 %reduce-scatter.5.cloned.1.call-start = ((), (), s32[]{:S(2)}) async-start(), calls=%async_computation.4 | async-start | bytes 2162688 | tf_op jit(solution)/shard_map/reduce_scatter | solution.py:152
  64.2 5.7 copy-start.3
  64.3 5.7 copy-start.8
  64.3 5.7 copy-start.9
  64.3 5.7 copy-start.12
  76.5 3.4 copy-start
  76.5 3.4 copy-start.10
  79.9 2.0 copy-start.2
  83.1 5.1 copy-start.1
  83.1 5.1 copy-start.11
  106.3 3.4 copy-start
  106.3 3.4 copy-start.10
  109.7 2.0 copy-start.2
  112.9 5.1 copy-start.1
  112.9 5.1 copy-start.11
  134.3 355.3 %reduce-scatter.3.cloned.1.call-start = ((), (), s32[]{:S(2)}) async-start(), calls=%async_computation.3 | async-start | bytes 2162688 | tf_op jit(solution)/shard_map/reduce_scatter | solution.py:146
  134.3 264.9 %copy-start.4 = (bf16[1,64,1024]{2,1,0:T(8,128)(2,1)S(1)}, bf16[1,64,1024]{2,1,0:T(8,128)(2,1)}, u32[]{:S(2)}) copy-start(bf16[1,64,1024]{2,1,0:T(8,128)(2,1)} %param.12) | copy-start | bytes 393220
  138.2 477.2 %all-reduce.8.cloned.1.call-start = ((), (), s32[]{:S(2)}) async-start(), calls=%async_computation.5 | async-start | bytes 8912896 | tf_op jit(solution)/shard_map/psum | solution.py:170
  492.2 203.9 %copy-start.7 = (bf16[64,512]{1,0:T(8,128)(2,1)S(1)}, bf16[64,512]{1,0:T(8,128)(2,1)}, u32[]{:S(2)}) copy-start(bf16[64,512]{1,0:T(8,128)(2,1)} %reduce-scatter.3.cloned.1.call-done) | copy-start | bytes 196612
  492.2 204.4 %copy-start.5 = (bf16[64,512]{1,0:T(8,128)(2,1)S(1)}, bf16[64,512]{1,0:T(8,128)(2,1)}, u32[]{:S(2)}) copy-start(bf16[64,512]{1,0:T(8,128)(2,1)} %reduce-scatter.5.cloned.1.call-done) | copy-start | bytes 196612
  492.2 240.1 %all-reduce.10.cloned.1.call-start = ((), (), s32[]{:S(2)}) async-start(), calls=%async_computation.6 | async-start | bytes 8912896 | tf_op jit(solution)/shard_map/psum | solution.py:171
  736.6 4.7 copy-start.6
Sparse Core Ops, SparseCore 0:
  10.5 53.6 all-gather.1
  134.4 264.7 reduce-scatter.4
  403.6 85.9 reduce-scatter.2
  493.7 121.6 all-reduce.7
  617.8 114.4 all-reduce.9
